TPU v7x, 32 devices: a whole 2x2x4 slice. The times are simulated.
32 devices in a mesh: seq: 8 (over y, x, core), head: 4 (over z).
Axes of the slice: x: 2, y: 2, z: 4, core: 2. Of those that a mesh axis runs over, the one named last changes fastest.
Arguments:
- out_grad: bfloat16 [2048, 4096], P('seq', 'head'), may hold values from -7.2 to 7.2
- x_in: bfloat16 [2048, 4096], P('seq', 'head'), may hold values from -6 to 6
- b_in: bfloat16 [2048, 128], P('seq'), may hold values from -2.5 to 2.5
- c_in: bfloat16 [2048, 128], P('seq'), may hold values from -2.5 to 2.5
- dt_raw: float32 [64, 2048], P('head', 'seq'), may hold values from -5.1 to -0.7
- dt_bias: float32 [64], P('head'), may hold values from -0.5 to 0.5
- a_log: float32 [64], P('head'), may hold values from -7.5 to 2.2
- d_skip: float32 [64], P('head'), may hold values from 0.5 to 1.5
- states: bfloat16 [8, 4096, 128], P('seq', 'head'), may hold values from -6 to 6
- w_out: bfloat16 [4096, 4096], P('head'), may hold values from -0.09375 to 0.09375
- w_in: bfloat16 [4096, 4096], P(None, 'head'), may hold values from -0.125 to 0.125
Outputs:
- in_grad: bfloat16 [4096, 2048], P('head', 'seq')
- bc_grad: bfloat16 [256, 2048], P('head', 'seq')
- dt_grad: float32 [64, 2048], P('head', 'seq')
- param_grad: float32 [3, 64], P(None, 'head')
All inputs are finite; a program needn't handle non-finite values.
Results may differ from a plain program's by a relative error of at most 0.015.
Values may be sent and summed in bfloat16 or wider, within the bound.
A program may use at most 64 MiB of HBM per device.

v0:
```python
import jax
import jax.numpy as jnp
from jax import lax
from jax.sharding import PartitionSpec as P


def entering(value, axis, join, neutral):
    count, mine = (lax.axis_size(axis), lax.axis_index(axis))
    pieces = jax.tree.map(lambda part: lax.all_gather(part, axis), value)
    pieces = jax.tree.map(lambda part: part[::-1], pieces)
    mine = count - 1 - mine
    so_far = jax.tree.map(
        lambda part, zero: jnp.full_like(part, 0) + jnp.asarray(zero, part.dtype), value, neutral
    )

    def turn(position, so_far):
        longer = join(so_far, jax.tree.map(lambda part: part[position], pieces))
        return jax.tree.map(lambda new, old: jnp.where(position < mine, new, old), longer, so_far)

    return lax.fori_loop(0, count - 1, turn, so_far)


def shards(out_grad, x_in, b_in, c_in, dt_raw, dt_bias, a_log, d_skip, states, w_out, w_in):
    tokens_here, inner_here = x_in.shape
    group_heads = dt_raw.shape[0]
    head_dim = inner_here // group_heads
    state_dim = b_in.shape[1]
    contract_last = (((1,), (1,)), ((), ()))
    head_sum = lax.dot_general(
        lax.all_gather(out_grad, "head", axis=1, tiled=True),
        w_out,
        contract_last,
        preferred_element_type=jnp.float32,
    )
    dy_heads = head_sum.astype(jnp.bfloat16).reshape(tokens_here, group_heads, head_dim)
    dy_wide = dy_heads.astype(jnp.float32)
    x_heads = x_in.reshape(tokens_here, group_heads, head_dim)
    x_wide = x_heads.astype(jnp.float32)
    decay_rate = jnp.exp(a_log)
    step_size = jax.nn.softplus(dt_raw + dt_bias[:, None])
    log_step = -decay_rate[:, None] * step_size
    cumlog = jnp.cumsum(log_step, axis=1)
    positions = jnp.arange(tokens_here)
    causal = positions[:, None] >= positions[None, :]
    log_gaps = cumlog[:, :, None] - cumlog[:, None, :]
    decay_mask = jnp.where(causal[None], jnp.exp(jnp.minimum(log_gaps, 0.0)), 0.0)
    scores = lax.dot_general(c_in, b_in, contract_last, preferred_element_type=jnp.float32)
    step_rows = step_size.T
    x_scaled = (x_wide * step_rows[:, :, None]).astype(jnp.bfloat16)
    pair_dots = jnp.einsum("ihp,jhp->hij", dy_heads, x_scaled, preferred_element_type=jnp.float32)
    kernel = (scores[None] * decay_mask).astype(jnp.bfloat16)
    intra_back = jnp.einsum("hij,ihp->jhp", kernel, dy_heads, preferred_element_type=jnp.float32)
    masked_dots = (pair_dots * decay_mask).astype(jnp.bfloat16)
    start_decay = jnp.exp(cumlog)
    dy_decay = (dy_wide * start_decay.T[:, :, None]).astype(jnp.bfloat16)
    local_state = jnp.einsum("ihp,in->hpn", dy_decay, c_in, preferred_element_type=jnp.float32)
    end_total = jnp.exp(cumlog[:, -1])
    entry_state = states.reshape(group_heads, head_dim, state_dim)
    db_intra = jnp.einsum("hij,in->nj", masked_dots, c_in, preferred_element_type=jnp.float32)
    dc_intra = jnp.einsum("hij,jn->ni", masked_dots, b_in, preferred_element_type=jnp.float32)
    dc_entry = jnp.einsum("ihp,hpn->ni", dy_decay, entry_state, preferred_element_type=jnp.float32)
    ystate = jnp.einsum("in,hpn->ihp", c_in, entry_state, preferred_element_type=jnp.float32)
    pair_weight = pair_dots * scores[None] * decay_mask
    state_terms = start_decay * jnp.sum(dy_wide * ystate, axis=2).T
    skip_terms = jnp.sum(dy_wide * x_wide, axis=(0, 2))

    def compose(earlier, nearer):
        return (nearer[0] * earlier[0], nearer[0][:, None, None] * earlier[1] + nearer[1])

    identity_pair = (jnp.ones_like(end_total), jnp.zeros_like(local_state))
    carried = entering((end_total, local_state), "seq", compose, identity_pair)[1]
    carried_bf = carried.astype(jnp.bfloat16)
    state_back = jnp.einsum("jn,hpn->jhp", b_in, carried_bf, preferred_element_type=jnp.float32)
    end_decay = jnp.exp(cumlog[:, -1:] - cumlog)
    end_weight = (step_size * end_decay).T
    x_grad = (
        (
            step_rows[:, :, None] * intra_back
            + end_weight[:, :, None] * state_back
            + d_skip[None, :, None] * dy_wide
        )
        .astype(jnp.bfloat16)
        .reshape(tokens_here, inner_here)
    )
    x_end = (x_wide * end_weight[:, :, None]).astype(jnp.bfloat16)
    db_entry = jnp.einsum("jhp,hpn->nj", x_end, carried_bf, preferred_element_type=jnp.float32)
    bc_part = jnp.concatenate([db_intra + db_entry, dc_intra + dc_entry], axis=0)
    end_terms = end_weight.T * jnp.sum(x_wide * state_back, axis=2).T
    cum_grad = pair_weight.sum(axis=2) - pair_weight.sum(axis=1) + state_terms - end_terms
    tail_grad = end_terms.sum(axis=1) + end_total * jnp.sum(
        entry_state.astype(jnp.float32) * carried, axis=(1, 2)
    )
    cum_grad = cum_grad.at[:, -1].add(tail_grad)
    step_grad = jnp.cumsum(cum_grad[:, ::-1], axis=1)[:, ::-1]
    dt_sum = (
        -decay_rate[:, None] * step_grad
        + jnp.sum(x_wide * (intra_back + end_decay.T[:, :, None] * state_back), axis=2).T
    )
    dt_grad = dt_sum * jax.nn.sigmoid(dt_raw + dt_bias[:, None])
    param_terms = jnp.stack(
        [jnp.sum(step_grad * log_step, axis=1), skip_terms, jnp.sum(dt_grad, axis=1)]
    )
    in_part = lax.psum_scatter(
        lax.dot_general(w_in, x_grad, contract_last, preferred_element_type=jnp.float32).astype(
            jnp.bfloat16
        ),
        "head",
        scatter_dimension=0,
        tiled=True,
    )
    bc_sum = lax.psum_scatter(bc_part.astype(jnp.bfloat16), "head", scatter_dimension=0, tiled=True)
    norm_scale = (lax.axis_size("seq") * tokens_here * head_dim) ** (-0.5)
    param_grad = lax.psum(param_terms, "seq") * norm_scale
    return (in_part, bc_sum, dt_grad, param_grad)


def solution(mesh):
    return jax.shard_map(
        shards,
        mesh=mesh,
        in_specs=(
            P("seq", "head"),
            P("seq", "head"),
            P("seq", None),
            P("seq", None),
            P("head", "seq"),
            P("head"),
            P("head"),
            P("head"),
            P("seq", "head", None),
            P("head", None),
            P(None, "head"),
        ),
        out_specs=(P("head", "seq"), P("head", "seq"), P("head", "seq"), P(None, "head")),
        check_vma=False,
    )
```

profile of v0, /device:TPU:0, one launch (start us, length us, event | category | flops | bytes accessed | tf_op | source)
XLA Modules:
  0.0 200.9 jit_solution(2288571976925971934)
XLA Ops:
  9.2 0.8 copy_bitcast_fusion.3
  11.0 1.4 fusion.35
  12.9 45.1 %all-gather.5.cloned.1.call-done = bf16[256,4096]{1,0:T(8,128)(2,1)} async-done(((bf16[256,1024]{1,0:T(8,128)(2,1)}), bf16[256,4096]{1,0:T(8,128)(2,1)}) %all-gather.5.cloned.1.call-update) | async-done | bytes 2097168 | tf_op jit(solution)/shard_map/all_gather | solution.py:30
  58.0 7.8 %fusion.17 = (f32[1024]{0:T(1024)}, bf16[256,1024]{1,0:T(8,128)(2,1)}, bf16[256,1024]{1,0:T(8,128)(2,1)S(1)}) fusion(bf16[256,1024]{1,0:T(8,128)(2,1)} %param.16, f32[256,1024]{1,0:T(8,128)S(1)} %copy.72, bf16[256,4096]{1,0:T(8,128)(2,1)} %all-gather.5.cloned.1.call-done, bf16[1024,4096]{1,0:T(8,128)(2,1)} %param.24), kind=kOutput, calls=%fused_computation.36 | convolution fusion | flops 2149317632 | bytes 13111296 | tf_op jit(solution)/shard_map/dot_general | solution.py:29
  66.0 1.1 fusion.22
  68.9 13.9 %all-reduce = f32[128]{0:T(128)S(1)} all-reduce(f32[128]{0:T(128)S(1)} %dynamic-update-slice.3), channel_id=2, replica_groups=mesh['seq'=8,'head'=4] {'seq'}, use_global_device_ids=true, to_apply=%add | all-reduce | flops 128 | bytes 1024
  84.1 2.0 fusion.10
  86.1 16.6 %all-gather.7.cloned.1.call-done = f32[128,64,128]{2,1,0:T(8,128)} async-done(((f32[16,64,128]{2,1,0:T(8,128)}), f32[128,64,128]{2,1,0:T(8,128)}) %all-gather.7.cloned.1.call-update) | async-done | bytes 4194320 | tf_op jit(solution)/shard_map/all_gather | solution.py:9
  102.8 4.7 %rev.13 = f32[8,16,64,128]{3,2,1,0:T(8,128)} reverse(f32[8,16,64,128]{3,2,1,0:T(8,128)} %bitcast.136), dimensions={0} | reverse | bytes 8388608 | tf_op jit(solution)/shard_map/rev | solution.py:10
  107.5 13.2 %while.15 = (s32[]{:T(128)}, f32[16,64,128]{2,1,0:T(8,128)S(1)}, s32[]{:T(128)}, f32[8,16]{1,0:T(8,128)}, f32[8,16,64,128]{3,2,1,0:T(8,128)}, /*index=5*/s32[]{:T(128)}, s32[]{:T(128)}) while((s32[]{:T(128)}, f32[16,64,128]{2,1,0:T(8,128)S(1)}, s32[]{:T(128)}, f32[8,16]{1,0:T(8,128)}, f32[8,16,64,128]{3,2,1,0:T(8,128)}, ...), condition=%wide.region_3.4_spmd.clone, body=%wide.region_2.3_spmd.clone.sunk | while | flops 524292 | bytes 1573161 | solution.py:20
  107.5 0.7 dynamic-slice_bitcast_fusion.2
  108.2 1.2 fusion.62
  109.4 0.7 dynamic-slice_bitcast_fusion.2
  110.1 1.2 fusion.62
  111.3 0.7 dynamic-slice_bitcast_fusion.2
  112.0 1.2 fusion.62
  113.2 0.7 dynamic-slice_bitcast_fusion.2
  113.9 1.2 fusion.62
  115.0 0.7 dynamic-slice_bitcast_fusion.2
  115.7 1.2 fusion.62
  116.9 0.7 dynamic-slice_bitcast_fusion.2
  117.6 1.2 fusion.62
  119.5 1.2 fusion.62
  120.7 1.2 multiply_reduce_fusion.1
  121.9 7.2 %fusion.1 = bf16[4096,256]{0,1:T(8,128)(2,1)} fusion(bf16[256,1024]{0,1:T(8,128)(2,1)S(1)} %bitcast.142, bf16[4096,1024]{1,0:T(8,128)(2,1)} %param.25), kind=kOutput, calls=%fused_computation.4 | convolution fusion | flops 2148532224 | bytes 11010048 | tf_op jit(solution)/shard_map/dot_general | solution.py:104
  129.3 0.7 reduce_sum.127
  131.0 3.5 %fusion.2 = (f32[16,256]{1,0:T(8,128)S(1)}, f32[16,256]{1,0:T(8,128)S(1)}, bf16[256,256]{1,0:T(8,128)(2,1)S(1)}) fusion(f32[16,256]{1,0:T(8,128)} %copy-done.13, f32[256,256]{1,0:T(8,128)} %copy-done.5, pred[256,256]{1,0:T(8,128)(4,1)} %copy-done.15, bf16[256,16,64]{0,2,1:T(8,128)(2,1)S(1)} %bitcast.135, f32[256,16,64]{0,2,1:T(8,128)S(1)} %bitcast.130, ...), kind=kOutput, calls=%fused_computation.10 | convolution fusion | flops 146202624 | bytes 2097152 | tf_op jit(solution)/shard_map/ihp,jhp->hij/dot_general | solution.py:50
  137.8 0.8 fusion.42
  138.7 13.9 %psum.7 = f32[3,16]{1,0:T(4,128)S(1)} all-reduce(f32[3,16]{1,0:T(4,128)S(1)} %pad_maximum_fusion.1), channel_id=1, replica_groups=mesh['seq'=8,'head'=4] {'seq'}, use_global_device_ids=true, to_apply=%region_20.21 | all-reduce | flops 48 | bytes 384 | tf_op jit(solution)/shard_map/psum | solution.py:113
  153.2 19.8 %reduce-scatter.3.cloned.1.call-done = bf16[1024,256]{0,1:T(8,128)(2,1)} async-done(((bf16[4096,256]{0,1:T(8,128)(2,1)}), bf16[1024,256]{0,1:T(8,128)(2,1)}) %reduce-scatter.3.cloned.1.call-update) | async-done | bytes 524304 | tf_op jit(solution)/shard_map/reduce_scatter | solution.py:103
  173.0 2.0 %copy.78 = bf16[1024,256]{1,0:T(8,128)(2,1)} copy(bf16[1024,256]{0,1:T(8,128)(2,1)} %reduce-scatter.3.cloned.1.call-done) | data formatting | bytes 1048576
  175.0 19.4 %reduce-scatter.5.cloned.1.call-done = bf16[64,256]{1,0:T(8,128)(2,1)} async-done(((bf16[256,256]{1,0:T(8,128)(2,1)}), bf16[64,256]{1,0:T(8,128)(2,1)}) %reduce-scatter.5.cloned.1.call-update) | async-done | bytes 32784 | tf_op jit(solution)/shard_map/reduce_scatter | solution.py:111
  (106 shorter events, 11.6 us)
Async XLA Ops:
  7.2 76.3 %copy-start = (bf16[256,128]{1,0:T(8,128)(2,1)S(1)}, bf16[256,128]{1,0:T(8,128)(2,1)}, u32[]{:S(2)}) copy-start(bf16[256,128]{1,0:T(8,128)(2,1)} %param.17) | copy-start | bytes 196612
  7.2 50.8 %all-gather.5.cloned.1.call-start = ((), (), s32[]{:S(2)}) async-start(), calls=%async_computation.2 | async-start | bytes 2621440 | tf_op jit(solution)/shard_map/all_gather | solution.py:30
  7.9 94.9 %all-gather.7.cloned.1.call-start = ((), (), s32[]{:S(2)}) async-start(), calls=%async_computation.5 | async-start | bytes 4718592 | tf_op jit(solution)/shard_map/all_gather | solution.py:9
  8.6 0.5 copy-start.22
  10.8 55.0 %copy-start.16 = (f32[16,2]{0,1:T(2,128)}, f32[16,2]{0,1:T(2,128)S(1)}, u32[]{:S(2)}) copy-start(f32[16,2]{0,1:T(2,128)S(1)} %slice.34) | copy-start | bytes 388
  10.8 1.6 copy-start.13
  11.0 54.8 %copy-start.19 = (f32[16]{0:T(128)}, f32[16]{0:T(128)S(1)}, u32[]{:S(2)}) copy-start(f32[16]{0:T(128)S(1)} %get-tuple-element.154) | copy-start | bytes 196
  12.9 53.1 %copy-start.2 = (bf16[256,128]{1,0:T(8,128)(2,1)S(1)}, bf16[256,128]{1,0:T(8,128)(2,1)}, u32[]{:S(2)}) copy-start(bf16[256,128]{1,0:T(8,128)(2,1)} %param.18) | copy-start | bytes 196612
  12.9 54.3 %copy-start.3 = (bf16[256,1024]{1,0:T(8,128)(2,1)S(1)}, bf16[256,1024]{1,0:T(8,128)(2,1)}, u32[]{:S(2)}) copy-start(bf16[256,1024]{1,0:T(8,128)(2,1)} %param.16) | copy-start | bytes 1572868
  65.8 1.6 copy-start.26
  67.2 105.8 %reduce-scatter.3.cloned.1.call-start = ((), (), s32[]{:S(2)}) async-start(), calls=%async_computation.3 | async-start | bytes 2621440 | tf_op jit(solution)/shard_map/reduce_scatter | solution.py:103
  83.5 0.6 copy-start.15
  84.1 23.4 %copy-start.5 = (f32[256,256]{1,0:T(8,128)}, f32[256,256]{1,0:T(8,128)S(1)}, u32[]{:S(2)}) copy-start(f32[256,256]{1,0:T(8,128)S(1)} %fusion.44) | copy-start | bytes 786436
  107.5 13.2 %copy-start.7 = (f32[256,16]{0,1:T(8,128)S(1)}, f32[256,16]{0,1:T(8,128)}, u32[]{:S(2)}) copy-start(f32[256,16]{0,1:T(8,128)} %get-tuple-element.175) | copy-start | bytes 49156
  107.5 13.2 %copy-start.9 = (f32[256,16]{0,1:T(8,128)S(1)}, f32[256,16]{0,1:T(8,128)}, u32[]{:S(2)}) copy-start(f32[256,16]{0,1:T(8,128)} %get-tuple-element.176) | copy-start | bytes 49156
  107.5 13.2 %copy-start.10 = (f32[256,16]{0,1:T(8,128)S(1)}, f32[256,16]{0,1:T(8,128)}, u32[]{:S(2)}) copy-start(f32[256,16]{0,1:T(8,128)} %get-tuple-element.174) | copy-start | bytes 49156
  107.5 13.2 %copy-start.25 = (f32[16]{0:T(128)S(1)}, f32[16]{0:T(128)}, u32[]{:S(2)}) copy-start(f32[16]{0:T(128)} %param.22) | copy-start | bytes 196
  121.9 7.3 %copy-start.21 = (f32[1024]{0:T(1024)S(1)}, f32[1024]{0:T(1024)}, u32[]{:S(2)}) copy-start(f32[1024]{0:T(1024)} %get-tuple-element.169) | copy-start | bytes 12292
  121.9 8.1 %copy-start.4 = (bf16[256,1024]{1,0:T(8,128)(2,1)S(1)}, bf16[256,1024]{1,0:T(8,128)(2,1)}, u32[]{:S(2)}) copy-start(bf16[256,1024]{1,0:T(8,128)(2,1)} %get-tuple-element.170) | copy-start | bytes 1572868
  121.9 8.3 %copy-start.1 = (bf16[1,1024,128]{2,1,0:T(8,128)(2,1)S(1)}, bf16[1,1024,128]{2,1,0:T(8,128)(2,1)}, u32[]{:S(2)}) copy-start(bf16[1,1024,128]{2,1,0:T(8,128)(2,1)} %param.23) | copy-start | bytes 786436
  129.2 65.2 %reduce-scatter.5.cloned.1.call-start = ((), (), s32[]{:S(2)}) async-start(), calls=%async_computation.4 | async-start | bytes 163840 | tf_op jit(solution)/shard_map/reduce_scatter | solution.py:111
  130.8 3.8 %copy-start.6 = (f32[16,256]{1,0:T(8,128)S(1)}, f32[16,256]{1,0:T(8,128)}, u32[]{:S(2)}) copy-start(f32[16,256]{1,0:T(8,128)} %param.19) | copy-start | bytes 49156
  130.9 3.8 %copy-start.11 = (f32[256,16]{0,1:T(8,128)S(1)}, f32[256,16]{0,1:T(8,128)}, u32[]{:S(2)}) copy-start(f32[256,16]{0,1:T(8,128)} %get-tuple-element.152) | copy-start | bytes 49156
  130.9 3.8 %copy-start.17 = (f32[16,2]{0,1:T(2,128)S(1)}, f32[16,2]{0,1:T(2,128)}, u32[]{:S(2)}) copy-start(f32[16,2]{0,1:T(2,128)} %copy-done.16) | copy-start | bytes 388
  130.9 3.8 %copy-start.18 = (f32[16]{0:T(128)S(1)}, f32[16]{0:T(128)}, u32[]{:S(2)}) copy-start(f32[16]{0:T(128)} %param.20) | copy-start | bytes 196
  130.9 3.8 %copy-start.20 = (f32[16]{0:T(128)S(1)}, f32[16]{0:T(128)}, u32[]{:S(2)}) copy-start(f32[16]{0:T(128)} %copy-done.19) | copy-start | bytes 196
  130.9 4.4 %copy-start.14 = (f32[16,256]{1,0:T(8,128)S(1)}, f32[16,256]{1,0:T(8,128)}, u32[]{:S(2)}) copy-start(f32[16,256]{1,0:T(8,128)} %copy-done.13) | copy-start | bytes 49156
  130.9 5.8 %copy-start.8 = (f32[256,16]{0,1:T(8,128)S(1)}, f32[256,16]{0,1:T(8,128)}, u32[]{:S(2)}) copy-start(f32[256,16]{0,1:T(8,128)} %get-tuple-element.175) | copy-start | bytes 49156
  130.9 6.9 %copy-start.12 = (f32[256,16]{0,1:T(8,128)S(1)}, f32[256,16]{0,1:T(8,128)}, u32[]{:S(2)}) copy-start(f32[256,16]{0,1:T(8,128)} %get-tuple-element.153) | copy-start | bytes 49156
  130.9 6.9 %copy-start.23 = (f32[16]{0:T(128)S(1)}, f32[16]{0:T(128)}, u32[]{:S(2)}) copy-start(f32[16]{0:T(128)} %copy-done.22) | copy-start | bytes 196
  130.9 7.7 %copy-start.24 = (f32[16]{0:T(128)S(1)}, f32[16]{0:T(128)}, u32[]{:S(2)}) copy-start(f32[16]{0:T(128)} %reduce_sum.127) | copy-start | bytes 196
Sparse Core Ops, SparseCore 0:
  9.6 48.3 all-gather.4
  67.3 35.4 all-gather.6
  129.3 43.6 reduce-scatter.2
  175.7 18.6 reduce-scatter.4
where the time goes:
time: 202 us; the launch traced here: 201 us
  waiting for transfers between devices  102 us (50%)
  blocking collectives  27.8 us (14%)
  matrix products  24.4 us (12%)
  local copies, waits for them, and re-layouts  16.4 us (8%)
  other arithmetic  15.7 us (8%)
  between operations  14.7 us (7%)
    all_gather x1, waiting for transfers between devices, shards(): lax.all_gather(out_grad, 'head', axis=1, tiled=True)  45.1 us
    reduce_scatter x1, waiting for transfers between devices, shards(): lax.psum_scatter(lax.dot_general(w_in, x_grad, contract_last, preferred_e...  19.8 us
    reduce_scatter x1, waiting for transfers between devices, shards(): lax.psum_scatter(bc_part.astype(jnp.bfloat16), 'head', scatter_dimension=...  19.4 us
    all_gather x1, waiting for transfers between devices, entering(): pieces = jax.tree.map(lambda part: lax.all_gather(part, axis), value)  16.6 us
    unnamed x1, blocking collectives  13.9 us
    psum x1, blocking collectives, shards(): param_grad = lax.psum(param_terms, 'seq') * norm_scale  13.9 us
    select_n x7, other arithmetic, turn(): jnp.where(position < mine, new, old)  8.18 us
    dot_general x1, matrix products, shards(): lax.dot_general(lax.all_gather(out_grad, 'head', axis=1, tiled=True), w_o...  7.83 us
  transfers between devices with their start and end apart: 4, of which 4 were waited for; matrix products, arithmetic and copies ran while one was open for 10% of the time, Pallas kernels for 0%

commit v1 on v0

--- a/solution.py
+++ b/solution.py
@@ -2,6 +2,14 @@
 import jax.numpy as jnp
 from jax import lax
 from jax.sharding import PartitionSpec as P
+
+
+def tiled_gather(value, axis, dim):
+    devices = lax.axis_size(axis)
+    repeats = [devices if d == dim else 1 for d in range(value.ndim)]
+    return lax.all_to_all(
+        jnp.tile(value, repeats), axis, split_axis=dim, concat_axis=dim, tiled=True
+    )
 
 
 def entering(value, axis, join, neutral):
@@ -27,10 +35,7 @@
     state_dim = b_in.shape[1]
     contract_last = (((1,), (1,)), ((), ()))
     head_sum = lax.dot_general(
-        lax.all_gather(out_grad, "head", axis=1, tiled=True),
-        w_out,
-        contract_last,
-        preferred_element_type=jnp.float32,
+        tiled_gather(out_grad, "head", 1), w_out, contract_last, preferred_element_type=jnp.float32
     )
     dy_heads = head_sum.astype(jnp.bfloat16).reshape(tokens_here, group_heads, head_dim)
     dy_wide = dy_heads.astype(jnp.float32)

time: 202 us -> 212 us (1.050)
  local copies, waits for them, and re-layouts: 16.4 us -> 23.2 us
  starting transfers between devices: 0.16 us -> 6.61 us
    all_gather x1 -> x0, waiting for transfers between devices: 45.1 us -> none  [shards(): lax.all_gather(out_grad, 'head', axis=1, tiled=True)]
    all_to_all x0 -> x1, waiting for transfers between devices: none -> 44.9 us  [tiled_gather(): lax.all_to_all(jnp.tile(value, repeats), axis, split_axis=dim, concat_axi...]
    all_to_all x0 -> x1, starting transfers between devices: none -> 6.35 us  [tiled_gather(): lax.all_to_all(jnp.tile(value, repeats), axis, split_axis=dim, concat_axi...]
    another operation x5 -> x6, local copies, waits for them, and re-layouts: 0.33 us -> 3.04 us  [the longest x1 2.7 us: tiled_gather(): jnp.tile(value, repeats)]
    all_to_all x0 -> x1, local copies, waits for them, and re-layouts: none -> 2.59 us  [tiled_gather(): lax.all_to_all(jnp.tile(value, repeats), axis, split_axis=dim, concat_axi...]
  transfers between devices with their start and end apart: 4 -> 4, of which waited for: 4 -> 4; matrix products, arithmetic and copies ran while one was open for 10% -> 9% of each run, Pallas kernels for 0% -> 0%
where the time goes in v1:
time: 212 us; the launch traced here: 210 us
  waiting for transfers between devices  101 us (48%)
  blocking collectives  27.3 us (13%)
  matrix products  24.5 us (12%)
  local copies, waits for them, and re-layouts  23.2 us (11%)
  between operations  14.7 us (7%)
  other arithmetic  13.6 us (6%)
  starting transfers between devices  6.61 us (3%)
    all_to_all x1, waiting for transfers between devices, tiled_gather(): lax.all_to_all(jnp.tile(value, repeats), axis, split_axis=dim, concat_axi...  44.9 us
    reduce_scatter x1, waiting for transfers between devices, shards(): lax.psum_scatter(lax.dot_general(w_in, x_grad, contract_last, preferred_e...  19.6 us
    reduce_scatter x1, waiting for transfers between devices, shards(): lax.psum_scatter(bc_part.astype(jnp.bfloat16), 'head', scatter_dimension=...  19.5 us
    all_gather x1, waiting for transfers between devices, entering(): pieces = jax.tree.map(lambda part: lax.all_gather(part, axis), value)  16.5 us
    psum x1, blocking collectives, shards(): param_grad = lax.psum(param_terms, 'seq') * norm_scale  13.9 us
    unnamed x1, blocking collectives  13.4 us
    select_n x7, other arithmetic, turn(): jnp.where(position < mine, new, old)  8.18 us
    dot_general x1, matrix products, shards(): lax.dot_general(tiled_gather(out_grad, 'head', 1), w_out, contract_last,...  7.92 us
  transfers between devices with their start and end apart: 4, of which 4 were waited for; matrix products, arithmetic and copies ran while one was open for 9% of the time, Pallas kernels for 0%

profile of v1, /device:TPU:0, one launch (start us, length us, event | category | flops | bytes accessed | tf_op | source)
XLA Modules:
  0.0 210.5 jit_solution(15616492040628268656)
XLA Ops:
  7.2 2.7 %tile.2 = bf16[256,4,1024]{2,0,1:T(8,128)(2,1)} broadcast(bf16[256,1024]{1,0:T(8,128)(2,1)} %param.15), dimensions={0,2} | broadcast | bytes 2621440 | tf_op jit(solution)/shard_map/tile | solution.py:11
  9.9 6.3 %all-to-all-start = ((bf16[256,4,1024]{2,0,1:T(8,128)(2,1)}), bf16[256,4,1024]{2,0,1:T(8,128)(2,1)S(1)}, u32[]{:S(2)}, u32[]{:S(2)}) async-start(bf16[256,4,1024]{2,0,1:T(8,128)(2,1)} %tile.2), calls=%async_computation | async-start | bytes 4194304 | tf_op jit(solution)/shard_map/all_to_all | solution.py:10
  17.5 0.7 fusion.35
  18.3 1.3 copy.85
  19.6 44.9 %all-to-all-done = bf16[256,4,1024]{2,0,1:T(8,128)(2,1)S(1)} async-done(((bf16[256,4,1024]{2,0,1:T(8,128)(2,1)}), bf16[256,4,1024]{2,0,1:T(8,128)(2,1)S(1)}, u32[]{:S(2)}, u32[]{:S(2)}) %all-to-all-start) | async-done | bytes 2097184 | tf_op jit(solution)/shard_map/all_to_all | solution.py:10
  64.5 2.6 %copy.80 = bf16[256,4,1024]{0,2,1:T(8,128)(2,1)} copy(bf16[256,4,1024]{2,0,1:T(8,128)(2,1)S(1)} %all-to-all-done) | data formatting | bytes 4194304 | tf_op jit(solution)/shard_map/all_to_all | solution.py:10
  67.1 7.9 %fusion.17 = (f32[1024]{0:T(1024)}, bf16[256,1024]{1,0:T(8,128)(2,1)}, bf16[256,1024]{1,0:T(8,128)(2,1)S(1)}) fusion(bf16[256,1024]{1,0:T(8,128)(2,1)} %param.16, f32[256,1024]{1,0:T(8,128)S(1)} %copy-done.1, bf16[256,4096]{0,1:T(8,128)(2,1)} %bitcast.140, bf16[1024,4096]{1,0:T(8,128)(2,1)} %param.24), kind=kOutput, calls=%fused_computation.36 | convolution fusion | flops 2149317632 | bytes 13111296 | tf_op jit(solution)/shard_map/dot_general | solution.py:37
  75.2 1.1 fusion.22
  76.4 1.2 copy.84
  79.0 13.4 %all-reduce = f32[128]{0:T(128)S(1)} all-reduce(f32[128]{0:T(128)S(1)} %dynamic-update-slice.3), channel_id=2, replica_groups=mesh['seq'=8,'head'=4] {'seq'}, use_global_device_ids=true, to_apply=%add | all-reduce | flops 128 | bytes 1024
  93.8 2.0 fusion.10
  95.8 16.5 %all-gather.4.cloned.1.call-done = f32[128,64,128]{2,1,0:T(8,128)} async-done(((f32[16,64,128]{2,1,0:T(8,128)}), f32[128,64,128]{2,1,0:T(8,128)}) %all-gather.4.cloned.1.call-update) | async-done | bytes 4194320 | tf_op jit(solution)/shard_map/all_gather | solution.py:17
  112.2 4.7 %rev.13 = f32[8,16,64,128]{3,2,1,0:T(8,128)} reverse(f32[8,16,64,128]{3,2,1,0:T(8,128)} %bitcast.137), dimensions={0} | reverse | bytes 8388608 | tf_op jit(solution)/shard_map/rev | solution.py:18
  117.0 13.2 %while.15 = (s32[]{:T(128)}, f32[16,64,128]{2,1,0:T(8,128)S(1)}, s32[]{:T(128)}, f32[8,16]{1,0:T(8,128)}, f32[8,16,64,128]{3,2,1,0:T(8,128)}, /*index=5*/s32[]{:T(128)}, s32[]{:T(128)}) while((s32[]{:T(128)}, f32[16,64,128]{2,1,0:T(8,128)S(1)}, s32[]{:T(128)}, f32[8,16]{1,0:T(8,128)}, f32[8,16,64,128]{3,2,1,0:T(8,128)}, ...), condition=%wide.region_3.4_spmd.clone, body=%wide.region_2.3_spmd.clone.sunk | while | flops 524292 | bytes 1573161 | solution.py:28
  117.0 0.7 dynamic-slice_bitcast_fusion.2
  117.7 1.2 fusion.62
  118.9 0.7 dynamic-slice_bitcast_fusion.2
  119.6 1.2 fusion.62
  121.4 1.2 fusion.62
  123.3 1.2 fusion.62
  125.2 1.2 fusion.62
  127.1 1.2 fusion.62
  129.0 1.2 fusion.62
  130.2 1.2 multiply_reduce_fusion.1
  131.4 7.2 %fusion.1 = bf16[4096,256]{0,1:T(8,128)(2,1)} fusion(bf16[256,1024]{0,1:T(8,128)(2,1)S(1)} %bitcast.144, bf16[4096,1024]{1,0:T(8,128)(2,1)} %param.25), kind=kOutput, calls=%fused_computation.4 | convolution fusion | flops 2148532224 | bytes 11010048 | tf_op jit(solution)/shard_map/dot_general | solution.py:109
  139.0 0.7 reduce_sum.127
  140.6 3.5 %fusion.2 = (f32[16,256]{1,0:T(8,128)S(1)}, f32[16,256]{1,0:T(8,128)S(1)}, bf16[256,256]{1,0:T(8,128)(2,1)S(1)}) fusion(f32[16,256]{1,0:T(8,128)} %copy-done.14, f32[256,256]{1,0:T(8,128)} %copy-done.5, pred[256,256]{1,0:T(8,128)(4,1)} %copy-done.16, bf16[256,16,64]{0,2,1:T(8,128)(2,1)S(1)} %bitcast.136, f32[256,16,64]{0,2,1:T(8,128)S(1)} %bitcast.131, ...), kind=kOutput, calls=%fused_computation.10 | convolution fusion | flops 146202624 | bytes 2097152 | tf_op jit(solution)/shard_map/ihp,jhp->hij/dot_general | solution.py:55
  147.5 0.8 fusion.42
  148.3 13.9 %psum.7 = f32[3,16]{1,0:T(4,128)S(1)} all-reduce(f32[3,16]{1,0:T(4,128)S(1)} %pad_maximum_fusion.1), channel_id=1, replica_groups=mesh['seq'=8,'head'=4] {'seq'}, use_global_device_ids=true, to_apply=%region_20.21 | all-reduce | flops 48 | bytes 384 | tf_op jit(solution)/shard_map/psum | solution.py:118
  162.8 19.6 %reduce-scatter.3.cloned.1.call-done = bf16[1024,256]{0,1:T(8,128)(2,1)} async-done(((bf16[4096,256]{0,1:T(8,128)(2,1)}), bf16[1024,256]{0,1:T(8,128)(2,1)}) %reduce-scatter.3.cloned.1.call-update) | async-done | bytes 524304 | tf_op jit(solution)/shard_map/reduce_scatter | solution.py:108
  182.5 2.0 copy.91
  184.5 19.5 %reduce-scatter.5.cloned.1.call-done = bf16[64,256]{1,0:T(8,128)(2,1)} async-done(((bf16[256,256]{1,0:T(8,128)(2,1)}), bf16[64,256]{1,0:T(8,128)(2,1)}) %reduce-scatter.5.cloned.1.call-update) | async-done | bytes 32784 | tf_op jit(solution)/shard_map/reduce_scatter | solution.py:116
  (113 shorter events, 12.2 us)
Async XLA Ops:
  7.2 86.0 %copy-start = (bf16[256,128]{1,0:T(8,128)(2,1)S(1)}, bf16[256,128]{1,0:T(8,128)(2,1)}, u32[]{:S(2)}) copy-start(bf16[256,128]{1,0:T(8,128)(2,1)} %param.17) | copy-start | bytes 196612
  7.2 9.1 %copy-start.28 = (f32[16]{0:T(128)S(1)}, f32[16]{0:T(128)}, u32[]{:S(2)}) copy-start(f32[16]{0:T(128)} %param.21) | copy-start | bytes 196
  7.2 9.1 %copy-start.6 = (f32[16,256]{1,0:T(8,128)S(1)}, f32[16,256]{1,0:T(8,128)}, u32[]{:S(2)}) copy-start(f32[16,256]{1,0:T(8,128)} %param.19) | copy-start | bytes 49156
  7.2 9.1 %copy-start.19 = (f32[16]{0:T(128)S(1)}, f32[16]{0:T(128)}, u32[]{:S(2)}) copy-start(f32[16]{0:T(128)} %param.20) | copy-start | bytes 196
  9.9 54.5 %all-to-all-start = ((bf16[256,4,1024]{2,0,1:T(8,128)(2,1)}), bf16[256,4,1024]{2,0,1:T(8,128)(2,1)S(1)}, u32[]{:S(2)}, u32[]{:S(2)}) async-start(bf16[256,4,1024]{2,0,1:T(8,128)(2,1)} %tile.2), calls=%async_computation | async-start | bytes 4194304 | tf_op jit(solution)/shard_map/all_to_all | solution.py:10
  16.3 96.0 %all-gather.4.cloned.1.call-start = ((), (), s32[]{:S(2)}) async-start(), calls=%async_computation.5 | async-start | bytes 4718592 | tf_op jit(solution)/shard_map/all_gather | solution.py:17
  16.3 1.9 copy-start.24
  17.2 57.8 %copy-start.17 = (f32[16,2]{0,1:T(2,128)}, f32[16,2]{0,1:T(2,128)S(1)}, u32[]{:S(2)}) copy-start(f32[16,2]{0,1:T(2,128)S(1)} %slice.34) | copy-start | bytes 388
  17.5 57.5 %copy-start.21 = (f32[16]{0:T(128)}, f32[16]{0:T(128)S(1)}, u32[]{:S(2)}) copy-start(f32[16]{0:T(128)S(1)} %get-tuple-element.158) | copy-start | bytes 196
  19.6 47.5 %copy-start.1 = (f32[256,1024]{1,0:T(8,128)S(1)}, f32[256,1024]{1,0:T(8,128)}, u32[]{:S(2)}) copy-start(f32[256,1024]{1,0:T(8,128)} %copy.85) | copy-start | bytes 3145732
  67.1 8.1 %copy-start.3 = (bf16[256,128]{1,0:T(8,128)(2,1)S(1)}, bf16[256,128]{1,0:T(8,128)(2,1)}, u32[]{:S(2)}) copy-start(bf16[256,128]{1,0:T(8,128)(2,1)} %param.18) | copy-start | bytes 196612
  75.0 2.7 %copy-start.29 = (u32[32]{0:T(128)S(1)}, u32[32]{0:T(128)}, u32[]{:S(2)}) copy-start(u32[32]{0:T(128)} %constant.78) | copy-start | bytes 388
  76.3 106.1 %reduce-scatter.3.cloned.1.call-start = ((), (), s32[]{:S(2)}) async-start(), calls=%async_computation.3 | async-start | bytes 2621440 | tf_op jit(solution)/shard_map/reduce_scatter | solution.py:108
  93.7 23.2 %copy-start.5 = (f32[256,256]{1,0:T(8,128)}, f32[256,256]{1,0:T(8,128)S(1)}, u32[]{:S(2)}) copy-start(f32[256,256]{1,0:T(8,128)S(1)} %fusion.44) | copy-start | bytes 786436
  116.9 13.2 %copy-start.8 = (f32[256,16]{0,1:T(8,128)S(1)}, f32[256,16]{0,1:T(8,128)}, u32[]{:S(2)}) copy-start(f32[256,16]{0,1:T(8,128)} %get-tuple-element.179) | copy-start | bytes 49156
  116.9 13.2 %copy-start.10 = (f32[256,16]{0,1:T(8,128)S(1)}, f32[256,16]{0,1:T(8,128)}, u32[]{:S(2)}) copy-start(f32[256,16]{0,1:T(8,128)} %get-tuple-element.180) | copy-start | bytes 49156
  117.0 13.2 %copy-start.11 = (f32[256,16]{0,1:T(8,128)S(1)}, f32[256,16]{0,1:T(8,128)}, u32[]{:S(2)}) copy-start(f32[256,16]{0,1:T(8,128)} %get-tuple-element.178) | copy-start | bytes 49156
  117.0 13.2 %copy-start.27 = (f32[16]{0:T(128)S(1)}, f32[16]{0:T(128)}, u32[]{:S(2)}) copy-start(f32[16]{0:T(128)} %param.22) | copy-start | bytes 196
  131.4 7.5 %copy-start.23 = (f32[1024]{0:T(1024)S(1)}, f32[1024]{0:T(1024)}, u32[]{:S(2)}) copy-start(f32[1024]{0:T(1024)} %get-tuple-element.173) | copy-start | bytes 12292
  131.4 8.3 %copy-start.4 = (bf16[256,1024]{1,0:T(8,128)(2,1)S(1)}, bf16[256,1024]{1,0:T(8,128)(2,1)}, u32[]{:S(2)}) copy-start(bf16[256,1024]{1,0:T(8,128)(2,1)} %get-tuple-element.174) | copy-start | bytes 1572868
  131.4 8.5 %copy-start.2 = (bf16[1,1024,128]{2,1,0:T(8,128)(2,1)S(1)}, bf16[1,1024,128]{2,1,0:T(8,128)(2,1)}, u32[]{:S(2)}) copy-start(bf16[1,1024,128]{2,1,0:T(8,128)(2,1)} %param.23) | copy-start | bytes 786436
  138.7 65.3 %reduce-scatter.5.cloned.1.call-start = ((), (), s32[]{:S(2)}) async-start(), calls=%async_computation.4 | async-start | bytes 163840 | tf_op jit(solution)/shard_map/reduce_scatter | solution.py:116
  140.5 3.8 %copy-start.7 = (f32[16,256]{1,0:T(8,128)S(1)}, f32[16,256]{1,0:T(8,128)}, u32[]{:S(2)}) copy-start(f32[16,256]{1,0:T(8,128)} %param.19) | copy-start | bytes 49156
  140.5 3.8 %copy-start.12 = (f32[256,16]{0,1:T(8,128)S(1)}, f32[256,16]{0,1:T(8,128)}, u32[]{:S(2)}) copy-start(f32[256,16]{0,1:T(8,128)} %get-tuple-element.156) | copy-start | bytes 49156
  140.5 3.8 %copy-start.18 = (f32[16,2]{0,1:T(2,128)S(1)}, f32[16,2]{0,1:T(2,128)}, u32[]{:S(2)}) copy-start(f32[16,2]{0,1:T(2,128)} %copy-done.17) | copy-start | bytes 388
  140.5 3.8 %copy-start.20 = (f32[16]{0:T(128)S(1)}, f32[16]{0:T(128)}, u32[]{:S(2)}) copy-start(f32[16]{0:T(128)} %param.20) | copy-start | bytes 196
  140.5 3.8 %copy-start.22 = (f32[16]{0:T(128)S(1)}, f32[16]{0:T(128)}, u32[]{:S(2)}) copy-start(f32[16]{0:T(128)} %copy-done.21) | copy-start | bytes 196
  140.5 4.4 %copy-start.15 = (f32[16,256]{1,0:T(8,128)S(1)}, f32[16,256]{1,0:T(8,128)}, u32[]{:S(2)}) copy-start(f32[16,256]{1,0:T(8,128)} %copy-done.14) | copy-start | bytes 49156
  140.6 5.8 %copy-start.9 = (f32[256,16]{0,1:T(8,128)S(1)}, f32[256,16]{0,1:T(8,128)}, u32[]{:S(2)}) copy-start(f32[256,16]{0,1:T(8,128)} %get-tuple-element.179) | copy-start | bytes 49156
  140.6 6.9 %copy-start.13 = (f32[256,16]{0,1:T(8,128)S(1)}, f32[256,16]{0,1:T(8,128)}, u32[]{:S(2)}) copy-start(f32[256,16]{0,1:T(8,128)} %get-tuple-element.157) | copy-start | bytes 49156
  140.6 6.9 %copy-start.25 = (f32[16]{0:T(128)S(1)}, f32[16]{0:T(128)}, u32[]{:S(2)}) copy-start(f32[16]{0:T(128)} %copy-done.24) | copy-start | bytes 196
  140.6 7.7 %copy-start.26 = (f32[16]{0:T(128)S(1)}, f32[16]{0:T(128)}, u32[]{:S(2)}) copy-start(f32[16]{0:T(128)} %reduce_sum.127) | copy-start | bytes 196
  (2 other events, 1.5 us)
Sparse Core Ops, SparseCore 0:
  76.4 35.7 all-gather.3
  138.8 43.6 reduce-scatter.2
  185.3 18.6 reduce-scatter.4
